TPU v7x, 32 devices: a whole 2x2x4 slice. The times are simulated.
32 devices in a mesh: prow: 4 (over y, x), pcol: 8 (over z, core).
Axes of the slice: x: 2, y: 2, z: 4, core: 2. Of those that a mesh axis runs over, the one named last changes fastest.
Arguments:
- schur: float32 [4, 4, 128, 2, 8, 128], P(None, 'prow', None, None, 'pcol'), may hold values from -0.125 to 0.125
- panel_inverse: float32 [2, 8, 128, 2, 4, 128], P(None, 'pcol', None, None, 'prow'), may hold values from -0.1875 to 0.1875
- coupling: float32 [4, 4, 128, 256], P(None, 'prow'), may hold values from -6 to 6
- zslab: float32 [4, 4, 128, 2, 8, 128], P(None, 'prow', None, None, 'pcol')
- targets: int32 [128], replicated, may hold values from 0 to 254
- pair_flags: int32 [128], replicated, may hold values 0 or 1
Outputs:
- eigenvectors: float32 [4, 4, 128, 128], P(None, 'prow', 'pcol')
All inputs are finite; a program needn't handle non-finite values.
Results may differ from a plain program's by a relative error of at most 0.0001.
Values sent between devices are 32-bit elements; how exact they have to be, the bound alone decides.
A program may use at most 64 MiB of HBM per device.

v0:
```python
import jax
import jax.numpy as jnp
from jax import lax
from jax.sharding import PartitionSpec as P

EPSILON = 1e-06


def shards(schur, panel_inverse, coupling, zslab, targets, pair_flags):
    block_size = schur.shape[2]
    row_blocks = schur.shape[0]
    col_blocks = schur.shape[3]
    ratio_rows = panel_inverse.shape[3]
    window = coupling.shape[3]
    vector_count = targets.shape[0]
    zrow_blocks = zslab.shape[0]
    panel_rows = ratio_rows * block_size
    triangle = schur.reshape(row_blocks * block_size, col_blocks * block_size)
    inverse = panel_inverse.reshape(col_blocks, block_size, panel_rows)
    strip_rows = coupling.reshape(row_blocks * block_size, window)
    z_rows = zslab.reshape(zrow_blocks * block_size, col_blocks * block_size)
    columns = jnp.arange(window, dtype=jnp.int32)[:, None]
    selection = (columns == targets[None, :]).astype(jnp.float32) + pair_flags[None, :].astype(
        jnp.float32
    ) * (columns == targets[None, :] + 1).astype(jnp.float32)
    right_side = -jnp.dot(strip_rows, selection, precision=lax.Precision.HIGHEST)
    pieces = [None] * col_blocks
    for panel_index in reversed(range(col_blocks)):
        residual = right_side[panel_index * panel_rows : (panel_index + 1) * panel_rows]
        if panel_index < col_blocks - 1:
            later_rows = jnp.concatenate(pieces[panel_index + 1 :], axis=0)
            partial_value = jnp.dot(
                triangle[
                    panel_index * panel_rows : (panel_index + 1) * panel_rows,
                    (panel_index + 1) * block_size :,
                ],
                later_rows,
                precision=lax.Precision.HIGHEST,
            )
            residual = residual - lax.psum(partial_value, "pcol")
        applied = jnp.dot(inverse[panel_index], residual, precision=lax.Precision.HIGHEST)
        pieces[panel_index] = lax.psum(applied, "prow")
    transformed = jnp.dot(z_rows, jnp.concatenate(pieces, axis=0), precision=lax.Precision.HIGHEST)
    stacked = transformed.reshape(zrow_blocks, 1, block_size, vector_count)
    total_rows = zrow_blocks * block_size * lax.axis_size("prow")
    summed = lax.psum(stacked, "pcol")
    squares = lax.psum(jnp.sum(summed * summed, axis=(0, 1, 2)), "prow")
    share_rows = block_size // lax.axis_size("pcol")
    owned_rows = lax.dynamic_slice_in_dim(
        summed, lax.axis_index("pcol") * share_rows, share_rows, 2
    )
    divisor = jnp.sqrt(squares / total_rows + EPSILON)
    return owned_rows / divisor[None, None, None, :]


def solution(mesh):
    in_specs = (
        P(None, "prow", None, None, "pcol", None),
        P(None, "pcol", None, None, "prow", None),
        P(None, "prow", None, None),
        P(None, "prow", None, None, "pcol", None),
        P(),
        P(),
    )
    out_specs = P(None, "prow", "pcol", None)
    return jax.shard_map(shards, mesh=mesh, in_specs=in_specs, out_specs=out_specs, check_vma=False)
```

profile of v0, /device:TPU:0, one launch (start us, length us, event | category | flops | bytes accessed | tf_op | source)
XLA Modules:
  0.0 233.2 jit_solution(16619724533023797762)
XLA Ops:
  6.5 0.0 copy-start
  6.5 0.0 copy-start.5
  6.5 0.0 all-reduce.5.cloned.1.call-start
  6.5 1.8 slice_reduce_fusion
  8.4 0.0 copy-done.5
  8.4 0.0 copy-start.4
  8.4 0.6 copy-done.4
  9.1 0.0 copy-done
  9.1 0.0 copy-start.2
  9.1 0.7 fusion
  9.8 0.9 convolution_bitcast_fusion.3
  10.7 0.0 all-reduce.5.cloned.1.call-update
  10.7 0.0 all-reduce.7.cloned.1.call-start
  10.8 0.0 copy-done.2
  10.8 0.0 copy-start.1
  10.8 44.6 %all-reduce.5.cloned.1.call-done = f32[128,128]{0,1:T(8,128)} async-done(((f32[128,128]{0,1:T(8,128)}), f32[128,128]{0,1:T(8,128)}) %all-reduce.5.cloned.1.call-update) | async-done | bytes 65552 | tf_op jit(solution)/shard_map/psum | solution.py:42
  55.4 1.8 convolution_bitcast_fusion.1
  57.2 0.0 all-reduce.7.cloned.1.call-update
  57.2 0.0 all-reduce.9.cloned.1.call-start
  57.3 55.4 %all-reduce.7.cloned.1.call-done = f32[256,128]{0,1:T(8,128)} async-done(((f32[256,128]{0,1:T(8,128)}), f32[256,128]{0,1:T(8,128)}) %all-reduce.7.cloned.1.call-update) | async-done | bytes 131088 | tf_op jit(solution)/shard_map/psum | solution.py:40
  112.7 1.8 convolution_bitcast_fusion.2
  114.5 0.0 copy-start.3
  114.5 0.0 all-reduce.9.cloned.1.call-update
  114.5 0.0 all-reduce.11.cloned.1.call-start
  114.5 41.9 %all-reduce.9.cloned.1.call-done = f32[128,128]{0,1:T(8,128)} async-done(((f32[128,128]{0,1:T(8,128)}), f32[128,128]{0,1:T(8,128)}) %all-reduce.9.cloned.1.call-update) | async-done | bytes 65552 | tf_op jit(solution)/shard_map/psum | solution.py:42
  156.5 0.0 copy-done.1
  156.5 0.0 copy-done.3
  156.5 1.5 convolution_bitcast_fusion
  158.0 0.8 copy.8
  158.8 0.0 all-reduce.11.cloned.1.call-update
  158.8 55.6 %all-reduce.11.cloned.1.call-done = f32[4,1,128,128]{3,2,1,0:T(8,128)} async-done(((f32[4,1,128,128]{3,2,1,0:T(8,128)}), f32[4,1,128,128]{3,2,1,0:T(8,128)}) %all-reduce.11.cloned.1.call-update) | async-done | bytes 262160 | tf_op jit(solution)/shard_map/psum | solution.py:46
  214.4 1.0 multiply_reduce_fusion
  215.4 9.8 %psum.39 = f32[128]{0:T(128)S(1)} all-reduce(f32[128]{0:T(128)S(1)} %multiply_reduce_fusion), channel_id=1, replica_groups=mesh['prow'=4,'pcol'=8] {'prow'}, use_global_device_ids=true, to_apply=%region_5.0 | all-reduce | flops 128 | bytes 1024 | tf_op jit(solution)/shard_map/psum | solution.py:47
  225.3 1.4 dynamic-slice_divide_fusion
  (4 shorter events, 0.1 us)
Async XLA Ops:
  6.5 2.5 %copy-start = (f32[4,1,128,256]{3,2,1,0:T(8,128)S(1)}, f32[4,1,128,256]{3,2,1,0:T(8,128)}, u32[]{:S(2)}) copy-start(f32[4,1,128,256]{3,2,1,0:T(8,128)} %param.8) | copy-start | bytes 1572868
  6.5 1.8 copy-start.5
  6.5 48.9 %all-reduce.5.cloned.1.call-start = ((), (), s32[]{:S(2)}) async-start(), calls=%async_computation | async-start | bytes 131072 | tf_op jit(solution)/shard_map/psum | solution.py:42
  8.4 0.7 copy-start.4
  9.1 1.7 copy-start.2
  10.7 102.0 %all-reduce.7.cloned.1.call-start = ((), (), s32[]{:S(2)}) async-start(), calls=%async_computation.1 | async-start | bytes 262144 | tf_op jit(solution)/shard_map/psum | solution.py:40
  10.8 145.7 %copy-start.1 = (f32[4,1,128,2,1,128]{5,4,3,2,1,0:T(1,128)S(1)}, f32[4,1,128,2,1,128]{5,4,3,2,1,0:T(1,128)}, u32[]{:S(2)}) copy-start(f32[4,1,128,2,1,128]{5,4,3,2,1,0:T(1,128)} %param.9) | copy-start | bytes 1572868
  57.2 99.3 %all-reduce.9.cloned.1.call-start = ((), (), s32[]{:S(2)}) async-start(), calls=%async_computation.2 | async-start | bytes 131072 | tf_op jit(solution)/shard_map/psum | solution.py:42
  114.5 42.0 %copy-start.3 = (f32[128,128]{0,1:T(8,128)S(1)}, f32[128,128]{0,1:T(8,128)}, u32[]{:S(2)}) copy-start(f32[128,128]{0,1:T(8,128)} %all-reduce.5.cloned.1.call-done) | copy-start | bytes 196612
  114.5 99.9 %all-reduce.11.cloned.1.call-start = ((), (), s32[]{:S(2)}) async-start(), calls=%async_computation.3 | async-start | bytes 524288 | tf_op jit(solution)/shard_map/psum | solution.py:46
Sparse Core Ops, SparseCore 0:
  10.8 44.5 all-reduce.4
  57.7 54.9 all-reduce.6
  115.5 40.8 all-reduce.8
  158.9 55.4 all-reduce.10
where the time goes:
time: 234 us; the launch traced here: 233 us
  waiting for transfers between devices  198 us (85%)
  between operations  13.2 us (6%)
  blocking collectives  9.84 us (4%)
  matrix products  6.66 us (3%)
  local copies, waits for them, and re-layouts  3.37 us (1%)
  other arithmetic  2.44 us (1%)
    psum x2, waiting for transfers between devices, shards(): pieces[panel_index] = lax.psum(applied, 'prow')  86.5 us
    psum x1, waiting for transfers between devices, shards(): summed = lax.psum(stacked, 'pcol')  55.6 us
    psum x1, waiting for transfers between devices, shards(): residual = residual - lax.psum(partial_value, 'pcol')  55.4 us
    psum x1, blocking collectives, shards(): squares = lax.psum(jnp.sum(summed * summed, axis=(0, 1, 2)), 'prow')  9.84 us
  transfers between devices with their start and end apart: 4, of which 4 were waited for; matrix products, arithmetic and copies ran while one was open for 0% of the time, Pallas kernels for 0%

commit v1 on v0

--- a/solution.py
+++ b/solution.py
@@ -37,7 +37,7 @@
                 later_rows,
                 precision=lax.Precision.HIGHEST,
             )
-            residual = residual - lax.psum(partial_value, "pcol")
+            residual = residual - jnp.sum(lax.all_gather(partial_value, "pcol"), axis=0)
         applied = jnp.dot(inverse[panel_index], residual, precision=lax.Precision.HIGHEST)
         pieces[panel_index] = lax.psum(applied, "prow")
     transformed = jnp.dot(z_rows, jnp.concatenate(pieces, axis=0), precision=lax.Precision.HIGHEST)

time: 234 us -> 201 us (0.86)
  waiting for transfers between devices: 198 us -> 164 us
    psum x1 -> x0, waiting for transfers between devices: 55.4 us -> none  [shards(): residual = residual - lax.psum(partial_value, 'pcol')]
    all_gather x0 -> x1, waiting for transfers between devices: none -> 22.4 us  [shards(): residual = residual - jnp.sum(lax.all_gather(partial_value, 'pcol'), axis=0)]
where the time goes in v1:
time: 201 us
  waiting for transfers between devices  164 us (82%)
  between operations  13.2 us (7%)
  blocking collectives  9.84 us (5%)
  matrix products  5.75 us (3%)
  local copies, waits for them, and re-layouts  4.93 us (2%)
  other arithmetic  2.69 us (1%)
    psum x2, waiting for transfers between devices, shards(): pieces[panel_index] = lax.psum(applied, 'prow')  86.1 us
    psum x1, waiting for transfers between devices, shards(): summed = lax.psum(stacked, 'pcol')  55.6 us
    all_gather x1, waiting for transfers between devices, shards(): residual = residual - jnp.sum(lax.all_gather(partial_value, 'pcol'), axis=0)  22.4 us
    psum x1, blocking collectives, shards(): squares = lax.psum(jnp.sum(summed * summed, axis=(0, 1, 2)), 'prow')  9.84 us
  transfers between devices with their start and end apart: 4, of which 4 were waited for; matrix products, arithmetic and copies ran while one was open for 0% of the time, Pallas kernels for 0%

profile of v1, /device:TPU:0, one launch (start us, length us, event | category | flops | bytes accessed | tf_op | source)
XLA Modules:
  0.0 200.7 jit_solution(12079543562359833911)
XLA Ops:
  6.5 0.0 copy-start
  6.5 0.0 copy-start.5
  6.5 0.0 all-reduce.4.cloned.1.call-start
  6.5 1.8 slice_reduce_fusion
  8.4 0.0 copy-done.5
  8.4 0.0 copy-start.4
  8.4 0.6 copy-done.4
  9.1 0.0 copy-done
  9.1 0.0 copy-start.2
  9.1 0.7 fusion
  9.8 0.9 convolution_bitcast_fusion.3
  10.7 0.0 all-reduce.4.cloned.1.call-update
  10.7 0.0 all-gather.3.cloned.1.call-start
  10.8 0.0 copy-done.2
  10.8 44.6 %all-reduce.4.cloned.1.call-done = f32[128,128]{0,1:T(8,128)} async-done(((f32[128,128]{0,1:T(8,128)}), f32[128,128]{0,1:T(8,128)}) %all-reduce.4.cloned.1.call-update) | async-done | bytes 65552 | tf_op jit(solution)/shard_map/psum | solution.py:42
  55.4 1.8 convolution_bitcast_fusion.1
  57.2 0.0 all-gather.3.cloned.1.call-update
  57.2 0.0 all-reduce.6.cloned.1.call-start
  57.2 22.4 %all-gather.3.cloned.1.call-done = f32[2048,128]{0,1:T(8,128)} async-done(((f32[256,128]{0,1:T(8,128)}), f32[2048,128]{0,1:T(8,128)}) %all-gather.3.cloned.1.call-update) | async-done | bytes 1048592 | tf_op jit(solution)/shard_map/all_gather | solution.py:40
  79.6 1.6 copy.11
  81.2 0.0 copy-start.3
  81.2 0.3 bitcast_reduce_fusion
  81.4 0.0 copy-start.1
  81.5 0.9 convolution_bitcast_fusion.2
  82.3 0.0 all-reduce.6.cloned.1.call-update
  82.4 0.0 all-reduce.8.cloned.1.call-start
  82.4 41.5 %all-reduce.6.cloned.1.call-done = f32[128,128]{0,1:T(8,128)} async-done(((f32[128,128]{0,1:T(8,128)}), f32[128,128]{0,1:T(8,128)}) %all-reduce.6.cloned.1.call-update) | async-done | bytes 65552 | tf_op jit(solution)/shard_map/psum | solution.py:42
  124.0 0.0 copy-done.3
  124.0 0.0 copy-done.1
  124.0 1.5 convolution_bitcast_fusion
  125.5 0.8 copy.8
  126.3 0.0 all-reduce.8.cloned.1.call-update
  126.3 55.6 %all-reduce.8.cloned.1.call-done = f32[4,1,128,128]{3,2,1,0:T(8,128)} async-done(((f32[4,1,128,128]{3,2,1,0:T(8,128)}), f32[4,1,128,128]{3,2,1,0:T(8,128)}) %all-reduce.8.cloned.1.call-update) | async-done | bytes 262160 | tf_op jit(solution)/shard_map/psum | solution.py:46
  181.9 1.0 multiply_reduce_fusion
  182.9 9.8 %psum.31 = f32[128]{0:T(128)S(1)} all-reduce(f32[128]{0:T(128)S(1)} %multiply_reduce_fusion), channel_id=1, replica_groups=mesh['prow'=4,'pcol'=8] {'prow'}, use_global_device_ids=true, to_apply=%region_5.0 | all-reduce | flops 128 | bytes 1024 | tf_op jit(solution)/shard_map/psum | solution.py:47
  192.8 1.4 dynamic-slice_divide_fusion
  (4 shorter events, 0.1 us)
Async XLA Ops:
  6.5 2.5 %copy-start = (f32[4,1,128,256]{3,2,1,0:T(8,128)S(1)}, f32[4,1,128,256]{3,2,1,0:T(8,128)}, u32[]{:S(2)}) copy-start(f32[4,1,128,256]{3,2,1,0:T(8,128)} %param.8) | copy-start | bytes 1572868
  6.5 1.8 copy-start.5
  6.5 48.9 %all-reduce.4.cloned.1.call-start = ((), (), s32[]{:S(2)}) async-start(), calls=%async_computation | async-start | bytes 131072 | tf_op jit(solution)/shard_map/psum | solution.py:42
  8.4 0.7 copy-start.4
  9.1 1.7 copy-start.2
  10.7 68.9 %all-gather.3.cloned.1.call-start = ((), (), s32[]{:S(2)}) async-start(), calls=%async_computation.3 | async-start | bytes 1179648 | tf_op jit(solution)/shard_map/all_gather | solution.py:40
  57.2 66.8 %all-reduce.6.cloned.1.call-start = ((), (), s32[]{:S(2)}) async-start(), calls=%async_computation.1 | async-start | bytes 131072 | tf_op jit(solution)/shard_map/psum | solution.py:42
  81.2 42.8 %copy-start.3 = (f32[128,128]{0,1:T(8,128)S(1)}, f32[128,128]{0,1:T(8,128)}, u32[]{:S(2)}) copy-start(f32[128,128]{0,1:T(8,128)} %all-reduce.4.cloned.1.call-done) | copy-start | bytes 196612
  81.4 42.5 %copy-start.1 = (f32[4,1,128,2,1,128]{5,4,3,2,1,0:T(1,128)S(1)}, f32[4,1,128,2,1,128]{5,4,3,2,1,0:T(1,128)}, u32[]{:S(2)}) copy-start(f32[4,1,128,2,1,128]{5,4,3,2,1,0:T(1,128)} %param.9) | copy-start | bytes 1572868
  82.4 99.5 %all-reduce.8.cloned.1.call-start = ((), (), s32[]{:S(2)}) async-start(), calls=%async_computation.2 | async-start | bytes 524288 | tf_op jit(solution)/shard_map/psum | solution.py:46
Sparse Core Ops, SparseCore 0:
  10.8 44.5 all-reduce.3
  57.3 22.2 all-gather.2
  82.5 41.4 all-reduce.5
  126.4 55.4 all-reduce.7
